TPU v7x, 32 devices: a whole 2x2x4 slice. The times are simulated.
32 devices in a mesh: groups: 2 (over x), expert: 8 (over z, y), wave: 2 (over core).
Axes of the slice: x: 2, y: 2, z: 4, core: 2. Of those that a mesh axis runs over, the one named last changes fastest.
Arguments:
- hidden_rows: bfloat16 [512, 2, 2048], P(('groups', 'expert', 'wave')), parts along dimension 0, may hold values from -6 to 6
- expert_ids: int32 [512, 2, 8], P(('groups', 'expert', 'wave')), parts along dimension 0, may hold values from 0 to 15, all different within a row; in each aligned block of 32 rows (0 to 31, 32 to 63, ..., all dimensions but the last counted through in order) at most 24 rows name the same one
- route_weights: float32 [512, 2, 8], P(('groups', 'expert', 'wave')), parts along dimension 0, may hold values from 0.1 to 1
- w_gate: bfloat16 [16, 2048, 768], P('expert', None, 'wave'), may hold values from -0.125 to 0.125
- w_up: bfloat16 [16, 2048, 768], P('expert', None, 'wave'), may hold values from -0.125 to 0.125
- w_down: bfloat16 [16, 768, 2048], P('expert', 'wave'), may hold values from -0.21875 to 0.21875
- codes: int32 [512, 2, 16], P(('groups', 'expert', 'wave')), parts along dimension 0, may hold values from 0 to 1023
- owner_slot: int32 [512], P(('groups', 'expert', 'wave')), parts along dimension 0, may hold values from 0 to 255, as said below
- code_table: bfloat16 [16, 1024, 1024], P(None, 'expert'), may hold values from -1.5 to 1.5
- conv_state: bfloat16 [512, 6, 1024], P(('groups', 'expert', 'wave')), parts along dimension 0, may hold values from -6 to 6
- conv_taps: float32 [7, 1024], replicated, may hold values from -2.4 to 2.4
- conv_bias: float32 [1024], replicated, may hold values from -3 to 3
- upsample: bfloat16 [1024, 512], replicated, may hold values from -0.1875 to 0.1875
Outputs:
- moe_out: bfloat16 [512, 2, 2048], P(('groups', 'expert', 'wave')), parts along dimension 0
- waveform: bfloat16 [512, 2, 512], P(('groups', 'expert', 'wave')), parts along dimension 0
- new_state: bfloat16 [512, 6, 1024], P(('groups', 'expert', 'wave')), parts along dimension 0
There are 2 independent parts, one for each index of `groups`. A program takes and returns all parts, laid end to end along the dimension named above; an argument that names none is the same for every part. Nothing has to cross between parts.
Inputs may be any that keep to these rules, and one draw needn't show every extreme that they name: `expert_ids`: each row names 8 different experts; among the 32 rows of one device no expert is named more than 24 times, a bound that some block reaches. `owner_slot`: A permutation of the slots. Slot o lies on the device holding rows o of the decoder's arrays; a session's slot lies on a device with the same index along wave as the session's own device, so every device holds 16 slots.
All inputs are finite; a program needn't handle non-finite values.
Results may differ from a plain program's by a relative error of at most 0.012.
Values may be sent and summed in bfloat16 or wider, within the bound.
A program may use at most 64 MiB of HBM per device.

v0:
```python
import jax
import jax.numpy as jnp
from jax import lax
from jax.sharding import PartitionSpec as P


def expert_work(received, w_gate, w_up, w_down):
    gate_val = jnp.einsum("secd,edf->secf", received, w_gate, preferred_element_type=jnp.float32)
    up_val = jnp.einsum("secd,edf->secf", received, w_up, preferred_element_type=jnp.float32)
    activated = (jax.nn.silu(gate_val) * up_val).astype(jnp.bfloat16)
    result = jnp.einsum("secf,efd->secd", activated, w_down, preferred_element_type=jnp.float32)
    return result.astype(jnp.bfloat16)


def mixture(hidden_rows, expert_ids, route_weights, w_gate, w_up, w_down):
    n_expert = lax.axis_size("expert")
    n_wave = lax.axis_size("wave")
    sessions_here, steps_count, width = hidden_rows.shape
    top_count = expert_ids.shape[2]
    local_experts = w_gate.shape[0]
    experts_all = n_expert * local_experts
    row_count = sessions_here * steps_count
    capacity = max(2, 3 * row_count * top_count // (2 * experts_all))
    tok_rows = hidden_rows.reshape(row_count, width)
    chosen = expert_ids.reshape(row_count * top_count)
    matches = (chosen[:, None] == jnp.arange(experts_all, dtype=jnp.int32)[None, :]).astype(
        jnp.int32
    )
    earlier = jnp.cumsum(matches, axis=0) - matches
    rank_in = jnp.sum(earlier * matches, axis=1)
    slot_index = chosen * capacity + rank_in
    slot_total = experts_all * capacity
    picker = (slot_index[:, None] == jnp.arange(slot_total, dtype=jnp.int32)[None, :]).astype(
        jnp.bfloat16
    )
    picker = jnp.sum(picker.reshape(row_count, top_count, slot_total), axis=1)
    outgoing = jnp.einsum("rs,rd->sd", picker, tok_rows, preferred_element_type=jnp.float32).astype(
        jnp.bfloat16
    )
    block_slots = local_experts * capacity
    outgoing = outgoing.reshape(n_expert, block_slots, width)
    arrived = lax.all_to_all(outgoing, "expert", split_axis=0, concat_axis=0, tiled=True)
    pooled = lax.all_gather(arrived, "wave", axis=0, tiled=True)
    partial_value = expert_work(
        pooled.reshape(n_wave * n_expert, local_experts, capacity, width), w_gate, w_up, w_down
    )
    own_half = lax.psum_scatter(
        partial_value.astype(jnp.float32)
        .reshape(n_wave * n_expert, block_slots, width)
        .astype(jnp.bfloat16),
        "wave",
        scatter_dimension=0,
        tiled=True,
    )
    slot_out = lax.all_to_all(own_half, "expert", split_axis=0, concat_axis=0, tiled=True)
    slot_flat = slot_out.reshape(slot_total, width)
    gathered_out = slot_flat[slot_index].astype(jnp.float32).reshape(row_count, top_count, width)
    mixed = jnp.sum(gathered_out * route_weights.reshape(row_count, top_count, 1), axis=1)
    return mixed.astype(jnp.bfloat16).reshape(sessions_here, steps_count, width)


def frames_path(codes, owner_slot, code_table, conv_state, conv_taps, conv_bias, upsample):
    n_expert = lax.axis_size("expert")
    n_wave = lax.axis_size("wave")
    sessions_here, frame_count, book_count = codes.shape
    shard_codes = code_table.shape[1]
    channels = code_table.shape[2]
    all_codes, all_owners = (
        lax.all_gather(codes, "expert", axis=0, tiled=True),
        lax.all_gather(owner_slot, "expert", axis=0, tiled=True),
    )
    position = all_owners // sessions_here // n_wave * sessions_here + all_owners % sessions_here
    ordered = jnp.zeros_like(all_codes).at[position].set(all_codes)
    shifted = ordered - lax.axis_index("expert") * shard_codes
    member = (shifted[..., None] == jnp.arange(shard_codes, dtype=jnp.int32)).astype(jnp.bfloat16)
    member = member.reshape(n_expert * sessions_here * frame_count, book_count * shard_codes)
    partial_value = jnp.dot(
        member,
        code_table.reshape(book_count * shard_codes, channels),
        preferred_element_type=jnp.float32,
    )
    frames = lax.psum_scatter(
        partial_value.reshape(n_expert * sessions_here, frame_count, channels).astype(jnp.bfloat16),
        "expert",
        scatter_dimension=0,
        tiled=True,
    ).astype(jnp.float32)
    history = jnp.concatenate([conv_state.astype(jnp.float32), frames], axis=1)
    state_len = conv_state.shape[1]
    kernel_len = conv_taps.shape[0]
    filtered = jnp.broadcast_to(conv_bias, frames.shape)
    for offset in range(kernel_len):
        filtered = (
            filtered
            + conv_taps[offset] * history[:, state_len - offset : state_len - offset + frame_count]
        )
    decoded = jax.nn.gelu(filtered).astype(jnp.bfloat16)
    samples = jnp.dot(
        decoded.reshape(sessions_here * frame_count, channels),
        upsample,
        preferred_element_type=jnp.float32,
    )
    samples = samples.astype(jnp.bfloat16).reshape(sessions_here, frame_count, upsample.shape[1])
    carried = history[:, frame_count:].astype(jnp.bfloat16)
    return (samples, carried)


def per_device(
    hidden_rows,
    expert_ids,
    route_weights,
    w_gate,
    w_up,
    w_down,
    codes,
    owner_slot,
    code_table,
    conv_state,
    conv_taps,
    conv_bias,
    upsample,
):
    mixed = mixture(hidden_rows, expert_ids, route_weights, w_gate, w_up, w_down)
    samples, carried = frames_path(
        codes, owner_slot, code_table, conv_state, conv_taps, conv_bias, upsample
    )
    return (mixed, samples, carried)


def solution(mesh):
    placed = (
        P(("groups", "expert", "wave"), None, None),
        P(("groups", "expert", "wave"), None, None),
        P(("groups", "expert", "wave"), None, None),
        P("expert", None, "wave"),
        P("expert", None, "wave"),
        P("expert", "wave", None),
        P(("groups", "expert", "wave"), None, None),
        P(("groups", "expert", "wave")),
        P(None, "expert", None),
        P(("groups", "expert", "wave"), None, None),
        P(),
        P(),
        P(),
    )
    return jax.shard_map(
        per_device,
        mesh=mesh,
        in_specs=placed,
        out_specs=(
            P(("groups", "expert", "wave"), None, None),
            P(("groups", "expert", "wave"), None, None),
            P(("groups", "expert", "wave"), None, None),
        ),
        check_vma=False,
    )
```

profile of v0, /device:TPU:0, one launch (start us, length us, event | category | flops | bytes accessed | tf_op | source)
XLA Modules:
  0.0 268.9 jit_solution(18359833729936917262)
XLA Ops:
  8.1 0.9 broadcast_multiply_fusion
  11.2 1.0 reshape.124
  12.8 44.2 %all_to_all.10 = bf16[8,48,2048]{2,1,0:T(8,128)(2,1)} all-to-all(bf16[8,48,2048]{2,1,0:T(8,128)(2,1)S(1)} %bitcast.94), channel_id=1, replica_groups=mesh['groups'=2,'expert'=8,'wave'=2] {'expert'}, dimensions={0} | all-to-all | bytes 3145728 | tf_op jit(solution)/shard_map/all_to_all | solution.py:42
  57.1 11.2 %all-gather.2.cloned.1.call-done = bf16[16,48,2048]{2,1,0:T(8,128)(2,1)} async-done(((bf16[8,48,2048]{2,1,0:T(8,128)(2,1)}), bf16[16,48,2048]{2,1,0:T(8,128)(2,1)}) %all-gather.2.cloned.1.call-update) | async-done | bytes 3145744 | tf_op jit(solution)/shard_map/all_gather | solution.py:43
  68.3 5.7 %fusion.13 = f32[16,2,24,384]{3,2,0,1:T(8,128)} fusion(bf16[2,2048,384]{2,1,0:T(8,128)(2,1)} %param.16, bf16[16,2,24,2048]{3,2,1,0:T(8,128)(2,1)} %bitcast.106), kind=kOutput, calls=%fused_computation.17 | convolution fusion | flops 1207959552 | bytes 7471104 | tf_op jit(solution)/shard_map/secd,edf->secf/dot_general | solution.py:8
  74.0 8.3 %fusion.7 = bf16[16,2,24,2048]{3,2,0,1:T(8,128)(2,1)} fusion(bf16[2,384,2048]{2,1,0:T(8,128)(2,1)S(1)} %copy-done, bf16[2,2048,384]{2,1,0:T(8,128)(2,1)} %param.17, bf16[16,2,24,2048]{3,2,1,0:T(8,128)(2,1)} %bitcast.107, f32[16,2,24,384]{3,2,0,1:T(8,128)} %fusion.13), kind=kOutput, calls=%fused_computation.10 | convolution fusion | flops 2419261440 | bytes 13762560 | tf_op jit(solution)/shard_map/secf,efd->secd/dot_general | solution.py:11
  82.3 4.0 %copy.54 = bf16[16,2,24,2048]{3,2,1,0:T(8,128)(2,1)} copy(bf16[16,2,24,2048]{3,2,0,1:T(8,128)(2,1)} %fusion.7) | data formatting | bytes 6291456 | tf_op jit(solution)/shard_map/convert_element_type | solution.py:12
  86.3 12.5 %reduce-scatter.3.cloned.1.call-done = bf16[8,48,2048]{2,1,0:T(8,128)(2,1)} async-done(((bf16[16,48,2048]{2,1,0:T(8,128)(2,1)}), bf16[8,48,2048]{2,1,0:T(8,128)(2,1)}) %reduce-scatter.3.cloned.1.call-update) | async-done | bytes 1572880 | tf_op jit(solution)/shard_map/reduce_scatter | solution.py:47
  98.8 5.9 %all-to-all-start.1 = ((bf16[8,48,2048]{2,1,0:T(8,128)(2,1)}), bf16[8,48,2048]{2,1,0:T(8,128)(2,1)}, u32[]{:S(2)}, u32[]{:S(2)}) async-start(bf16[8,48,2048]{2,1,0:T(8,128)(2,1)} %reduce-scatter.3.cloned.1.call-done), calls=%async_computation.2 | async-start | bytes 3145728 | tf_op jit(solution)/shard_map/all_to_all | solution.py:55
  106.3 36.0 %all-reduce = s32[128]{0:T(128)S(1)} all-reduce(s32[128]{0:T(128)S(1)} %dynamic-update-slice), channel_id=1, replica_groups=mesh['groups'=2,'expert'=8,'wave'=2] {'expert'}, use_global_device_ids=true, to_apply=%add | all-reduce | flops 128 | bytes 1024
  142.3 30.7 %all_gather.11 = s32[128,2,16]{2,1,0:T(2,128)S(1)} all-gather(s32[16,2,16]{2,1,0:T(2,128)S(1)} %copy-done.2), channel_id=1, replica_groups=mesh['groups'=2,'expert'=8,'wave'=2] {'expert'}, dimensions={0}, use_global_device_ids=true | all-gather | bytes 18432 | tf_op jit(solution)/shard_map/all_gather | solution.py:69
  173.0 4.3 %scatter_fusion = s32[128,2,16]{2,1,0:T(2,128)S(1)} fusion(s32[128,2,16]{2,1,0:T(2,128)S(1)} %broadcast_in_dim.7, s32[128]{0:T(128)S(1)} %compare_select_fusion.1, s32[128,2,16]{2,1,0:T(2,128)S(1)} %all_gather.11), kind=kCustom, calls=%fused_computation.1 | custom fusion | bytes 49664 | tf_op jit(solution)/shard_map/scatter | solution.py:73
  177.5 4.3 %fusion.36 = bf16[128,2,1024]{2,0,1:T(8,128)(2,1)} fusion(bf16[16,128,1024]{2,1,0:T(8,128)(2,1)} %param.21, s32[128,2,16]{0,2,1:T(8,128)S(1)} %broadcast_subtract_fusion), kind=kOutput, calls=%fused_computation.22 | convolution fusion | flops 1074528256 | bytes 4734976 | tf_op jit(solution)/shard_map/dot_general | solution.py:77
  182.5 1.0 convert_element_type.75
  184.8 1.6 fusion.70
  186.4 57.2 %reduce-scatter.5.cloned.1.call-done = bf16[16,2,1024]{2,0,1:T(8,128)(2,1)} async-done(((bf16[128,2,1024]{2,0,1:T(8,128)(2,1)}), bf16[16,2,1024]{2,0,1:T(8,128)(2,1)}) %reduce-scatter.5.cloned.1.call-update) | async-done | bytes 65552 | tf_op jit(solution)/shard_map/reduce_scatter | solution.py:82
  243.7 0.8 convert_element_type.74
  245.2 0.9 fusion.55
  246.7 1.5 reshape.128
  248.2 2.2 convolution_convert_fusion.2
  250.4 1.4 reshape.129
  251.8 1.6 fusion.45
  253.4 5.1 %gather_fusion = bf16[256,2048]{1,0:T(8,128)(2,1)} fusion(bf16[384,2048]{1,0:T(8,128)(2,1)} %bitcast.14, s32[1024]{0:T(1024)} %pad_clamp_fusion), kind=kCustom, calls=%fused_computation | custom fusion | bytes 2098176 | tf_op jit(solution)/shard_map/gather | solution.py:57
  258.4 2.2 fusion.12
  (48 shorter events, 8.2 us)
Async XLA Ops:
  8.0 66.0 %copy-start = (bf16[2,384,2048]{2,1,0:T(8,128)(2,1)S(1)}, bf16[2,384,2048]{2,1,0:T(8,128)(2,1)}, u32[]{:S(2)}) copy-start(bf16[2,384,2048]{2,1,0:T(8,128)(2,1)} %param.18) | copy-start | bytes 9437188
  8.0 60.3 %all-gather.2.cloned.1.call-start = ((), (), s32[]{:S(2)}) async-start(), calls=%async_computation.4 | async-start | bytes 4718592 | tf_op jit(solution)/shard_map/all_gather | solution.py:43
  10.9 46.1 %copy-start.3 = (s32[256]{0:T(256)}, s32[256]{0:T(256)S(1)}, u32[]{:S(2)}) copy-start(s32[256]{0:T(256)S(1)} %fusion.66) | copy-start | bytes 3076
  57.0 41.7 %reduce-scatter.3.cloned.1.call-start = ((), (), s32[]{:S(2)}) async-start(), calls=%async_computation.5 | async-start | bytes 4718592 | tf_op jit(solution)/shard_map/reduce_scatter | solution.py:47
  86.3 18.5 %copy-start.6 = (u32[32]{0:T(128)S(1)}, u32[32]{0:T(128)}, u32[]{:S(2)}) copy-start(u32[32]{0:T(128)} %constant.84) | copy-start | bytes 388
  86.3 19.7 %copy-start.5 = (s32[16]{0:T(128)S(1)}, s32[16]{0:T(128)}, u32[]{:S(2)}) copy-start(s32[16]{0:T(128)} %param.20) | copy-start | bytes 196
  86.3 56.0 %copy-start.2 = (s32[16,2,16]{2,1,0:T(2,128)S(1)}, s32[16,2,16]{2,1,0:T(2,128)}, u32[]{:S(2)}) copy-start(s32[16,2,16]{2,1,0:T(2,128)} %param.19) | copy-start | bytes 6148
  98.8 154.6 %all-to-all-start.1 = ((bf16[8,48,2048]{2,1,0:T(8,128)(2,1)}), bf16[8,48,2048]{2,1,0:T(8,128)(2,1)}, u32[]{:S(2)}, u32[]{:S(2)}) async-start(bf16[8,48,2048]{2,1,0:T(8,128)(2,1)} %reduce-scatter.3.cloned.1.call-done), calls=%async_computation.2 | async-start | bytes 3145728 | tf_op jit(solution)/shard_map/all_to_all | solution.py:55
  104.7 139.0 %reduce-scatter.5.cloned.1.call-start = ((), (), s32[]{:S(2)}) async-start(), calls=%async_computation.6 | async-start | bytes 589824 | tf_op jit(solution)/shard_map/reduce_scatter | solution.py:82
  177.4 5.0 %copy-start.4 = (f32[16,2,8]{0,2,1:T(8,128)S(1)}, f32[16,2,8]{0,2,1:T(8,128)}, u32[]{:S(2)}) copy-start(f32[16,2,8]{0,2,1:T(8,128)} %param.15) | copy-start | bytes 3076
  244.5 0.7 copy-start.1
Sparse Core Ops, SparseCore 0:
  57.2 11.1 all-gather.1
  86.4 12.3 reduce-scatter.2
Sparse Core Ops, SparseCore 1:
  181.9 61.7 reduce-scatter.4
where the time goes:
time: 270 us; the launch traced here: 269 us
  blocking collectives  111 us (41%)
  waiting for transfers between devices  81 us (30%)
  local copies, waits for them, and re-layouts  24 us (9%)
  matrix products  21.1 us (8%)
  between operations  16.3 us (6%)
  other arithmetic  9.58 us (4%)
  starting transfers between devices  6.02 us (2%)
    reduce_scatter x1, waiting for transfers between devices, frames_path(): lax.psum_scatter(partial_value.reshape(n_expert * sessions_here, frame_co...  57.2 us
    all_to_all x1, blocking collectives, mixture(): lax.all_to_all(outgoing, 'expert', split_axis=0, concat_axis=0, tiled=True)  44.2 us
    unnamed x1, blocking collectives  36 us
    all_gather x1, blocking collectives, frames_path(): lax.all_gather(codes, 'expert', axis=0, tiled=True)  30.7 us
    reduce_scatter x1, waiting for transfers between devices, mixture(): lax.psum_scatter(partial_value.astype(jnp.float32).reshape(n_wave * n_exp...  12.5 us
    all_gather x1, waiting for transfers between devices, mixture(): pooled = lax.all_gather(arrived, 'wave', axis=0, tiled=True)  11.2 us
    dot_general x1, matrix products, expert_work(): jnp.einsum('secf,efd->secd', activated, w_down, preferred_element_type=jn...  8.29 us
    all_to_all x1, starting transfers between devices, mixture(): lax.all_to_all(own_half, 'expert', split_axis=0, concat_axis=0, tiled=True)  5.9 us
  transfers between devices with their start and end apart: 4, of which 3 were waited for; matrix products, arithmetic and copies ran while one was open for 9% of the time, Pallas kernels for 0%

commit v1 on v0

v1 whole, which is shorter than its diff:
```python
import functools

import jax
import jax.numpy as jnp
from jax import lax
from jax.experimental import pallas as pl
from jax.experimental.pallas import tpu as pltpu
from jax.sharding import PartitionSpec as P

MESH = pl.DeviceIdType.MESH
BF = jnp.bfloat16
F32 = jnp.float32
RADIX = 64
LANES = 128


def dot(a, b):
    return jnp.dot(a, b, preferred_element_type=F32)


def kernel(
    n_e, n_w, inner, experts, books, scales,
    x_ref, wg_ref, wu_ref, wd_ref, tab_ref,
    moe_ref, fr_ref,
    xg, wgu, wdv, tabv, mem, act,
    psend, precv, pown, ps, my, ma, mz,
    fs, fy, fa, fz,
    w_sem, zu_sem, zd_sem, ys_sem, ws_sem, ag_recv,
    p_sem, mys, myr, mzs, mzr, fys, fyr, fzs, fzr,
):
    outer = n_e // inner
    rows = x_ref.shape[0]
    width = moe_ref.shape[1]
    channels = fr_ref.shape[1]
    local = wg_ref.shape[0]
    units = wg_ref.shape[2]
    shard = tab_ref.shape[0] // books
    wave_rows = n_e * rows
    e = lax.axis_index("expert")
    w = lax.axis_index("wave")
    z = e // inner
    y = e % inner
    peer = 1 - w
    ye = z * inner + (inner - 1 - y)

    def remote(src, dst, ssem, rsem, te, tw):
        return pltpu.make_async_remote_copy(
            src_ref=src, dst_ref=dst, send_sem=ssem, recv_sem=rsem,
            device_id={"expert": te, "wave": tw}, device_id_type=MESH,
        )

    loads = []
    loads.append(pltpu.make_async_copy(tab_ref, tabv, w_sem.at[0]))
    for j in range(local):
        loads.append(pltpu.make_async_copy(wg_ref.at[j], wgu.at[j, :, pl.ds(0, units)], w_sem.at[1 + 2 * j]))
        loads.append(pltpu.make_async_copy(wu_ref.at[j], wgu.at[j, :, pl.ds(units, units)], w_sem.at[2 + 2 * j]))
    loads.append(pltpu.make_async_copy(wd_ref, wdv, w_sem.at[1 + 2 * local]))

    barrier = pltpu.get_barrier_semaphore()

    def greet(te, tw):
        pl.semaphore_signal(barrier, inc=1, device_id={"expert": te, "wave": tw}, device_id_type=MESH)

    greet(e, peer)
    if inner == 2:
        greet(ye, w)
    for d in range(1, outer):
        greet((z + d) % outer * inner + y, w)
    pl.semaphore_wait(barrier, 1 + (inner - 1) + (outer - 1))

    def slot(te, tw):
        return xg.at[pl.ds((tw * n_e + te) * rows, rows), :]

    def up(src, zo):
        te = zo * inner + y
        return remote(src, slot(te, w), zu_sem.at[zo], ag_recv.at[w * n_e + te], (z + 1) * inner + y, w)

    def down(src, zo):
        te = zo * inner + y
        return remote(src, slot(te, w), zd_sem.at[zo], ag_recv.at[w * n_e + te], (z - 1) * inner + y, w)

    def across(src, zo):
        te = zo * inner + y
        return remote(src, slot(te, w), ys_sem.at[zo], ag_recv.at[w * n_e + te], ye, w)

    def over(src, te):
        return remote(src, slot(te, w), ws_sem.at[te], ag_recv.at[w * n_e + te], e, peer)

    def arrived(te, tw):
        remote(slot(te, tw), slot(te, tw), ws_sem.at[te], ag_recv.at[tw * n_e + te], e, peer).wait_recv()

    @pl.when(z + 1 < outer)
    def _():
        up(x_ref, z).start()

    @pl.when(z > 0)
    def _():
        down(x_ref, z).start()

    if inner == 2:
        across(x_ref, z).start()
    over(x_ref, e).start()
    for load in loads:
        load.start()
    xg[pl.ds((w * n_e + e) * rows, rows), :] = x_ref[...]

    def spread(zo):
        te = zo * inner + y
        if inner == 2:
            across(slot(te, w), zo).start()
        over(slot(te, w), te).start()

    def from_across(zo):
        te = zo * inner + (inner - 1 - y)
        arrived(te, w)
        over(slot(te, w), te).start()

    def both_sides(step, act_on):
        @pl.when(z - step >= 0)
        def _():
            act_on(z - step)

        @pl.when(z + step < outer)
        def _():
            act_on(z + step)

    for step in range(1, outer):
        @pl.when(z - step >= 0)
        def _():
            zo = z - step
            te = zo * inner + y
            arrived(te, w)

            @pl.when(z + 1 < outer)
            def _():
                up(slot(te, w), zo).start()

            spread(zo)

        @pl.when(z + step < outer)
        def _():
            zo = z + step
            te = zo * inner + y
            arrived(te, w)

            @pl.when(z > 0)
            def _():
                down(slot(te, w), zo).start()

            spread(zo)

        if inner == 2:
            if step == 1:
                from_across(z)
            else:
                both_sides(step - 1, from_across)
    if inner == 2:
        if outer == 1:
            from_across(z)
        else:
            both_sides(outer - 1, from_across)

    def small(tw):
        extra = xg[pl.ds(pl.multiple_of(tw * wave_rows, wave_rows), wave_rows), width:]
        lanes = extra.shape[1]
        src = lax.broadcasted_iota(jnp.int32, (lanes, LANES), 0)
        col = lax.broadcasted_iota(jnp.int32, (lanes, LANES), 1)
        code_at = 2 * experts
        dest_at = code_at + 2 * books
        is_code = col < books
        pick = jnp.where(is_code & (src == code_at + col), float(RADIX), 0.0)
        pick += jnp.where(is_code & (src == code_at + books + col), 1.0, 0.0)
        pick += jnp.where((col == books) & (src == dest_at), float(RADIX), 0.0)
        pick += jnp.where((col == books) & (src == dest_at + 1), 1.0, 0.0)
        own = e * local + col - (books + 1)
        is_weight = (col > books) & (col <= books + local)
        pick += jnp.where(is_weight & ((src == own) | (src == own + experts)), 1.0, 0.0)
        return dot(extra, pick.astype(BF))

    said = small(w)
    lane = lax.broadcasted_iota(jnp.int32, (wave_rows, shard), 1).astype(F32)
    first = (e * shard).astype(F32)
    for q in range(books):
        mem[:, q * shard:(q + 1) * shard] = jnp.where(
            said[:, q:q + 1] - first == lane, 1.0, 0.0
        ).astype(BF)
    place = lax.broadcasted_iota(jnp.int32, (wave_rows, wave_rows), 1).astype(F32)
    order = jnp.where(said[:, books:books + 1] == place, 1.0, 0.0).astype(BF)
    loads[0].wait()
    f_tile = min(channels, 512)

    @pl.loop(0, channels // f_tile)
    def _(n):
        cols = pl.ds(pl.multiple_of(n * f_tile, f_tile), f_tile)
        part = dot(mem[...], tabv[:, cols]).astype(BF)
        fs[:, cols] = lax.dot_general(
            order, part, (((0,), (0,)), ((), ())), preferred_element_type=F32
        ).astype(BF)

    turns = sorted(range(1, outer), key=lambda d: -min(d, outer - d)) + [0]

    def block(zo, yo):
        return pl.ds(pl.multiple_of((zo * inner + yo) * rows, rows), rows)

    def zrows(zo):
        return pl.ds(pl.multiple_of(zo * rows, rows), rows)

    def y_copy(src, dst, ss, rs, zo):
        return remote(src.at[block(zo, 1 - y), :], dst.at[zrows(zo), :], ss.at[zo], rs.at[zo], ye, w)

    def z_copy(src, dst, ss, rs, d):
        zo = (z + d) % outer
        return remote(src.at[zrows(zo), :], dst.at[zrows(d - 1), :], ss.at[d - 1], rs.at[d - 1], zo * inner + y, w)

    def f_start():
        if inner == 2:
            for d in turns:
                y_copy(fs, fy, fys, fyr, (z + d) % outer).start()

    def f_middle():
        for d in turns:
            zo = (z + d) % outer
            total = fs[block(zo, y), :].astype(F32)
            if inner == 2:
                y_copy(fs, fy, fys, fyr, zo).wait_recv()
                total += fy[zrows(zo), :].astype(F32)
            if d:
                fa[zrows(zo), :] = total.astype(BF)
                z_copy(fa, fz, fzs, fzr, d).start()
            else:
                fr_ref[...] = total

    f_start()

    def chunk(tw, dst):
        x = xg[pl.ds(pl.multiple_of(tw * wave_rows, wave_rows), wave_rows), :width]
        told = small(tw)
        for j in range(local):
            gu = dot(x, wgu[j])
            g = gu[:, :units]
            u = gu[:, units:]
            a = g / (1.0 + jnp.exp(-g)) * u * told[:, books + 1 + j:books + 2 + j]
            act[:, j * units:(j + 1) * units] = a.astype(BF)
        tile = min(width, 512)

        @pl.loop(0, width // tile)
        def _(n):
            cols = pl.ds(pl.multiple_of(n * tile, tile), tile)
            dst[:, cols] = dot(act[...], wdv[:, cols]).astype(BF)

    @pl.loop(0, n_e)
    def _(te):
        arrived(te, peer)

    for load in loads[1:]:
        load.wait()
    chunk(peer, psend)
    swap = remote(psend, precv, p_sem.at[0], p_sem.at[1], e, peer)
    swap.start()
    f_middle()
    chunk(w, pown)
    swap.wait_recv()

    if inner == 2:
        for d in turns:
            zo = (z + d) % outer
            there = block(zo, 1 - y)
            ps[there, :] = (pown[there, :].astype(F32) + precv[there, :].astype(F32)).astype(BF)
            y_copy(ps, my, mys, myr, zo).start()
    mine = None
    for d in turns:
        zo = (z + d) % outer
        here = block(zo, y)
        total = pown[here, :].astype(F32) + precv[here, :].astype(F32)
        if inner == 2:
            y_copy(ps, my, mys, myr, zo).wait_recv()
            total += my[zrows(zo), :].astype(F32)
        if d:
            ma[zrows(zo), :] = total.astype(BF)
            z_copy(ma, mz, mzs, mzr, d).start()
        else:
            mine = total
    for d in turns[:-1]:
        z_copy(fa, fz, fzs, fzr, d).wait_recv()
        fr_ref[...] += fz[zrows(d - 1), :].astype(F32)
    for d in turns[:-1]:
        z_copy(ma, mz, mzs, mzr, d).wait_recv()
        mine += mz[zrows(d - 1), :].astype(F32)
    moe_ref[...] = mine.astype(BF)

    for zo in range(outer):
        @pl.when((z + 1 < outer) & (zo <= z))
        def _():
            up(x_ref, zo).wait_send()

        @pl.when((z > 0) & (zo >= z))
        def _():
            down(x_ref, zo).wait_send()

        if inner == 2:
            across(x_ref, zo).wait_send()
            y_copy(fs, fy, fys, fyr, zo).wait_send()
            y_copy(ps, my, mys, myr, zo).wait_send()
    for d in turns[:-1]:
        z_copy(fa, fz, fzs, fzr, d).wait_send()
        z_copy(ma, mz, mzs, mzr, d).wait_send()

    @pl.loop(0, n_e)
    def _(te):
        over(x_ref, te).wait_send()

    swap.wait_send()


def exchange(packed, w_gate, w_up, w_down, table, width, experts, books):
    n_e = lax.axis_size("expert")
    n_w = lax.axis_size("wave")
    inner = 2 if n_e % 2 == 0 else 1
    outer = n_e // inner
    rows = packed.shape[0]
    local, _, units = w_gate.shape
    channels = table.shape[1]
    wave_rows = n_e * rows
    vm = pltpu.VMEM
    dma = lambda *s: pltpu.SemaphoreType.DMA(s)
    hops = max(outer - 1, 1)
    scratch = [
        vm((n_w * wave_rows, packed.shape[1]), BF),
        vm((local, width, 2 * units), BF),
        vm((local * units, width), BF),
        vm(table.shape, BF),
        vm((wave_rows, table.shape[0]), BF),
        vm((wave_rows, local * units), BF),
        vm((wave_rows, width), BF),
        vm((wave_rows, width), BF),
        vm((wave_rows, width), BF),
        vm((wave_rows, width), BF),
        vm((outer * rows, width), BF),
        vm((outer * rows, width), BF),
        vm((hops * rows, width), BF),
        vm((wave_rows, channels), BF),
        vm((outer * rows, channels), BF),
        vm((outer * rows, channels), BF),
        vm((hops * rows, channels), BF),
        dma(2 + 2 * local), dma(outer), dma(outer), dma(outer), dma(n_e), dma(n_w * n_e),
        dma(2), dma(outer), dma(outer), dma(hops), dma(hops),
        dma(outer), dma(outer), dma(hops), dma(hops),
    ]
    any_spec = pl.BlockSpec(memory_space=pl.ANY)
    vm_spec = pl.BlockSpec(memory_space=pltpu.VMEM)
    return pl.pallas_call(
        functools.partial(kernel, n_e, n_w, inner, experts, books, None),
        out_shape=(
            jax.ShapeDtypeStruct((rows, width), BF),
            jax.ShapeDtypeStruct((rows, channels), F32),
        ),
        in_specs=[vm_spec] + [any_spec] * 4,
        out_specs=(vm_spec, vm_spec),
        scratch_shapes=scratch,
        compiler_params=pltpu.CompilerParams(
            collective_id=0, has_side_effects=True, vmem_limit_bytes=60 * 1024 * 1024
        ),
    )(packed, w_gate, w_up, w_down, table)


def per_device(
    hidden_rows, expert_ids, route_weights, w_gate, w_up, w_down,
    codes, owner_slot, code_table, conv_state, conv_taps, conv_bias, upsample,
):
    n_e = lax.axis_size("expert")
    n_w = lax.axis_size("wave")
    sessions, steps, width = hidden_rows.shape
    rows = sessions * steps
    top = expert_ids.shape[2]
    experts = n_e * w_gate.shape[0]
    books, shard, channels = code_table.shape

    ids = expert_ids.reshape(rows, top)
    names = jnp.arange(experts, dtype=jnp.int32)
    weight = jnp.sum(
        jnp.where(ids[:, :, None] == names, route_weights.reshape(rows, top, 1), 0.0), axis=1
    )
    high = lax.reduce_precision(weight, 8, 7)
    dest = owner_slot // sessions // n_w * sessions + owner_slot % sessions
    dest = (dest[:, None] * steps + jnp.arange(steps, dtype=jnp.int32)).reshape(rows, 1)
    code_rows = codes.reshape(rows, books)
    used = 2 * experts + 2 * books + 2
    extra = jnp.concatenate(
        [
            high.astype(BF),
            (weight - high).astype(BF),
            (code_rows // RADIX).astype(BF),
            (code_rows % RADIX).astype(BF),
            (dest // RADIX).astype(BF),
            (dest % RADIX).astype(BF),
            jnp.zeros((rows, -used % LANES), BF),
        ],
        axis=1,
    )
    packed = jnp.concatenate([hidden_rows.reshape(rows, width), extra], axis=1)
    moe, frames = exchange(
        packed, w_gate, w_up, w_down.reshape(-1, width),
        code_table.reshape(books * shard, channels), width, experts, books,
    )
    frames = frames.reshape(sessions, steps, channels)
    history = jnp.concatenate([conv_state.astype(F32), frames], axis=1)
    state_len = conv_state.shape[1]
    filtered = jnp.broadcast_to(conv_bias, frames.shape)
    for offset in range(conv_taps.shape[0]):
        filtered = filtered + conv_taps[offset] * history[:, state_len - offset:state_len - offset + steps]
    decoded = jax.nn.gelu(filtered).astype(BF)
    samples = jnp.dot(decoded.reshape(rows, channels), upsample, preferred_element_type=F32)
    samples = samples.astype(BF).reshape(sessions, steps, upsample.shape[1])
    carried = history[:, steps:].astype(BF)
    return moe.reshape(sessions, steps, width), samples, carried


def solution(mesh):
    rows = P(("groups", "expert", "wave"), None, None)
    placed = (
        rows, rows, rows,
        P("expert", None, "wave"), P("expert", None, "wave"), P("expert", "wave", None),
        rows, P(("groups", "expert", "wave")), P(None, "expert", None), rows, P(), P(), P(),
    )
    return jax.shard_map(
        per_device, mesh=mesh, in_specs=placed, out_specs=(rows, rows, rows), check_vma=False
    )
```

time: 270 us -> 59.9 us (0.22)
  blocking collectives: 111 us -> 0 us
  waiting for transfers between devices: 81 us -> 0 us
  Pallas kernels: 0 us -> 49 us
  matrix products: 21.1 us -> 0.27 us
  local copies, waits for them, and re-layouts: 24 us -> 7.21 us
  between operations: 16.3 us -> 0.75 us
  other arithmetic: 9.58 us -> 2.4 us
  starting transfers between devices: 6.02 us -> 0 us
    reduce_scatter x2 -> x0, waiting for transfers between devices: 69.7 us -> none  [the longest x1 57.2 us: frames_path(): lax.psum_scatter(partial_value.reshape(n_expert * sessions_here, frame_co...]
    pallas_call x0 -> x1, Pallas kernels: none -> 49 us  [exchange(): pl.pallas_call(functools.partial(kernel, n_e, n_w, inner, experts, books,...]
    all_to_all x1 -> x0, blocking collectives: 44.2 us -> none  [mixture(): lax.all_to_all(outgoing, 'expert', split_axis=0, concat_axis=0, tiled=True)]
    unnamed x1 -> x0, blocking collectives: 36 us -> none
    all_gather x1 -> x0, blocking collectives: 30.7 us -> none  [frames_path(): lax.all_gather(codes, 'expert', axis=0, tiled=True)]
    dot_general x5 -> x1, matrix products: 21.1 us -> 0.27 us  [per_device(): jnp.dot(decoded.reshape(rows, channels), upsample, preferred_element_type...]
    all_gather x1 -> x0, waiting for transfers between devices: 11.2 us -> none  [mixture(): pooled = lax.all_gather(arrived, 'wave', axis=0, tiled=True)]
    all_to_all x1 -> x0, starting transfers between devices: 5.9 us -> none  [mixture(): lax.all_to_all(own_half, 'expert', split_axis=0, concat_axis=0, tiled=True)]
  transfers between devices with their start and end apart: 4 -> 0, of which waited for: 3 -> 0; matrix products, arithmetic and copies ran while one was open for 9% -> 0% of each run, Pallas kernels for 0% -> 0%
where the time goes in v1:
time: 59.9 us; the launch traced here: 59.6 us
  Pallas kernels  49 us (82%)
  local copies, waits for them, and re-layouts  7.21 us (12%)
  other arithmetic  2.4 us (4%)
  between operations  0.75 us (1%)
    pallas_call x1, Pallas kernels, exchange(): pl.pallas_call(functools.partial(kernel, n_e, n_w, inner, experts, books,...  49 us
    reshape x1, local copies, waits for them, and re-layouts, per_device(): return (moe.reshape(sessions, steps, width), samples, carried)  1.66 us
    unnamed x10, local copies, waits for them, and re-layouts  1.58 us

profile of v1, /device:TPU:0, one launch (start us, length us, event | category | flops | bytes accessed | tf_op | source)
XLA Modules:
  0.0 59.6 jit_solution(2490469541348235485)
XLA Ops:
  0.6 0.0 copy-start
  0.6 1.0 %reshape.201 = bf16[32,2048]{1,0:T(8,128)(2,1)S(1)} reshape(bf16[16,2,2048]{2,1,0:T(2,128)(2,1)} %param.13) | data formatting | bytes 262144 | tf_op jit(solution)/shard_map/reshape | solution.py:400
  1.7 0.8 %copy.46 = f32[16,2,8]{2,1,0:T(2,128)S(1)} copy(f32[16,2,8]{0,2,1:T(8,128)} %param.15) | data formatting | bytes 2048 | tf_op args[2]
  2.5 0.1 copy.47
  2.5 0.8 %copy.44 = s32[16,2,8]{2,1,0:T(2,128)S(1)} copy(s32[16,2,8]{0,2,1:T(8,128)} %param.14) | data formatting | bytes 2048 | tf_op args[1]
  3.3 0.1 copy.45
  3.4 0.1 copy.49
  3.5 0.1 copy.48
  3.6 0.7 %fusion.18 = (bf16[32,16]{1,0:T(8,128)(2,1)S(1)}, bf16[32,16]{1,0:T(8,128)(2,1)S(1)}) fusion(s32[32,16]{1,0:T(8,128)} %bitcast.25), kind=kLoop, calls=%fused_computation.40 | loop fusion | flops 10752 | bytes 4096 | tf_op jit(solution)/shard_map/convert_element_type | solution.py:393
  4.3 0.7 %fusion.26 = s32[16]{0:T(128)S(1)} fusion(s32[16]{0:T(128)} %param.20), kind=kLoop, calls=%fused_computation.61 | loop fusion | flops 592 | bytes 128 | tf_op jit(solution)/shard_map/mul | solution.py:385
  5.0 0.1 iota_add_fusion
  5.1 0.1 add.130
  5.2 0.8 %concatenate.6.x_ref = bf16[32,2176]{1,0:T(8,128)(2,1)} concatenate(bf16[32,2048]{1,0:T(8,128)(2,1)S(1)} %reshape.201, bf16[32,16]{1,0:T(8,128)(2,1)S(1)} %get-tuple-element.19, bf16[32,16]{1,0:T(8,128)(2,1)S(1)} %get-tuple-element.18, bf16[32,16]{1,0:T(8,128)(2,1)S(1)} %get-tuple-element.17, bf16[32,16]{1,0:T(8,128)(2,1)S(1)} %get-tuple-element.16, ...), dimensions={1} | concatenate | bytes 278528 | tf_op jit(solution)/shard_map/concatenate | solution.py:400
  6.0 49.0 %shard_map.148 = (bf16[32,2048]{1,0:T(8,128)(2,1)}, f32[32,1024]{1,0:T(8,128)}) custom-call(bf16[32,2176]{1,0:T(8,128)(2,1)} %concatenate.6.x_ref, bf16[2,2048,384]{2,1,0:T(8,128)(2,1)} %wg_ref.1, bf16[2,2048,384]{2,1,0:T(8,128)(2,1)} %wu_ref.1, bf16[768,2048]{1,0:T(8,128)(2,1)} %bitcast.15, bf16[2048,1024]{1,0:T(8,128)(2,1)} %bitcast.14), custom_call_target="tpu_custom_call" | custom-call | tf_op jit(solution)/shard_map/pallas_call | solution.py:351
  54.9 1.7 %reshape.205 = bf16[16,2,2048]{2,1,0:T(2,128)(2,1)} reshape(bf16[32,2048]{1,0:T(8,128)(2,1)} %get-tuple-element.5) | data formatting | bytes 262144 | tf_op jit(solution)/shard_map/reshape | solution.py:415
  56.6 0.0 copy-done.1
  56.6 1.0 %reshape.206 = f32[16,2,1024]{2,1,0:T(2,128)S(1)} reshape(f32[32,1024]{1,0:T(8,128)} %get-tuple-element.6) | data formatting | bytes 262144 | tf_op jit(solution)/shard_map/reshape | solution.py:405
  57.7 0.0 copy-done.2
  57.7 0.0 copy-done.3
  57.7 0.1 fusion.8
  57.8 0.1 copy.57
  58.0 0.3 convolution_convert_fusion
  58.2 0.7 %reshape.208 = bf16[16,2,512]{2,1,0:T(2,128)(2,1)} reshape(bf16[32,512]{1,0:T(8,128)(2,1)S(1)} %convolution_convert_fusion) | data formatting | bytes 65536 | tf_op jit(solution)/shard_map/reshape | solution.py:413
  58.9 0.7 %fusion = bf16[16,6,1024]{2,0,1:T(8,128)(2,1)} fusion(f32[16,2,1024]{2,0,1:T(8,128)S(1)} %copy.55, f32[16,6,1024]{2,0,1:T(8,128)S(1)} %convert_element_type.50), kind=kLoop, calls=%fused_computation.4 | loop fusion | flops 98304 | bytes 720896 | tf_op jit(solution)/shard_map/convert
  (13 shorter events, 0.2 us)
Async XLA Ops:
  0.6 57.3 %copy-start = (bf16[1024,512]{1,0:T(8,128)(2,1)S(1)}, bf16[1024,512]{1,0:T(8,128)(2,1)}, u32[]{:S(2)}) copy-start(bf16[1024,512]{1,0:T(8,128)(2,1)} %param.25) | copy-start | bytes 3145732
  6.0 50.6 %copy-start.1 = (bf16[16,6,1024]{2,0,1:T(8,128)(2,1)S(1)}, bf16[16,6,1024]{2,0,1:T(8,128)(2,1)}, u32[]{:S(2)}) copy-start(bf16[16,6,1024]{2,0,1:T(8,128)(2,1)} %param.22) | copy-start | bytes 589828
  6.0 51.7 %copy-start.2 = (f32[7,1024]{1,0:T(8,128)S(1)}, f32[7,1024]{1,0:T(8,128)}, u32[]{:S(2)}) copy-start(f32[7,1024]{1,0:T(8,128)} %param.23) | copy-start | bytes 86020
  6.0 51.8 %copy-start.3 = (f32[1024]{0:T(1024)S(1)}, f32[1024]{0:T(1024)}, u32[]{:S(2)}) copy-start(f32[1024]{0:T(1024)} %param.24) | copy-start | bytes 12292

commit v2 on v1

--- a/solution.py
+++ b/solution.py
@@ -19,13 +19,13 @@
 
 
 def kernel(
-    n_e, n_w, inner, experts, books, scales,
+    n_e, n_w, inner, experts, books,
     x_ref, wg_ref, wu_ref, wd_ref, tab_ref,
     moe_ref, fr_ref,
     xg, wgu, wdv, tabv, mem, act,
-    psend, precv, pown, ps, my, ma, mz,
+    part, precv, ps, my, ma, mz,
     fs, fy, fa, fz,
-    w_sem, zu_sem, zd_sem, ys_sem, ws_sem, ag_recv,
+    w_sem, zu_sem, ys_sem, ws_sem, ag_recv,
     p_sem, mys, myr, mzs, mzr, fys, fyr, fzs, fzr,
 ):
     outer = n_e // inner
@@ -36,6 +36,9 @@
     units = wg_ref.shape[2]
     shard = tab_ref.shape[0] // books
     wave_rows = n_e * rows
+    halves = 2 if outer > 1 and outer & (outer - 1) == 0 else 1
+    half_e = n_e // halves
+    half_rows = half_e * rows
     e = lax.axis_index("expert")
     w = lax.axis_index("wave")
     z = e // inner
@@ -61,23 +64,34 @@
     def greet(te, tw):
         pl.semaphore_signal(barrier, inc=1, device_id={"expert": te, "wave": tw}, device_id_type=MESH)
 
+    power = outer & (outer - 1) == 0
+
+    def far(k):
+        if not power:
+            return (z + k) % outer, (z - k + outer) % outer
+        flipped = z
+        bit = 1
+        while bit < outer:
+            if k & bit:
+                flipped = flipped + bit - 2 * bit * (z // bit % 2)
+            bit *= 2
+        return flipped, flipped
+
     greet(e, peer)
     if inner == 2:
         greet(ye, w)
-    for d in range(1, outer):
-        greet((z + d) % outer * inner + y, w)
+    for k in range(1, outer):
+        greet(far(k)[0] * inner + y, w)
     pl.semaphore_wait(barrier, 1 + (inner - 1) + (outer - 1))
 
+    def start_row(te, tw):
+        return ((te // half_e * n_w + tw) * half_e + te % half_e) * rows
+
     def slot(te, tw):
-        return xg.at[pl.ds((tw * n_e + te) * rows, rows), :]
-
-    def up(src, zo):
-        te = zo * inner + y
-        return remote(src, slot(te, w), zu_sem.at[zo], ag_recv.at[w * n_e + te], (z + 1) * inner + y, w)
-
-    def down(src, zo):
-        te = zo * inner + y
-        return remote(src, slot(te, w), zd_sem.at[zo], ag_recv.at[w * n_e + te], (z - 1) * inner + y, w)
+        return xg.at[pl.ds(pl.multiple_of(start_row(te, tw), rows), rows), :]
+
+    def along(k):
+        return remote(x_ref, slot(e, w), zu_sem.at[k], ag_recv.at[w * n_e + e], far(k)[0] * inner + y, w)
 
     def across(src, zo):
         te = zo * inner + y
@@ -89,79 +103,36 @@
     def arrived(te, tw):
         remote(slot(te, tw), slot(te, tw), ws_sem.at[te], ag_recv.at[tw * n_e + te], e, peer).wait_recv()
 
-    @pl.when(z + 1 < outer)
-    def _():
-        up(x_ref, z).start()
-
-    @pl.when(z > 0)
-    def _():
-        down(x_ref, z).start()
-
+    if outer > 1:
+        along(1).start()
     if inner == 2:
         across(x_ref, z).start()
     over(x_ref, e).start()
+    for k in range(2, outer):
+        along(k).start()
     for load in loads:
         load.start()
-    xg[pl.ds((w * n_e + e) * rows, rows), :] = x_ref[...]
-
-    def spread(zo):
-        te = zo * inner + y
-        if inner == 2:
-            across(slot(te, w), zo).start()
+    xg[pl.ds(pl.multiple_of(start_row(e, w), rows), rows), :] = x_ref[...]
+
+    def spread(k):
+        te = far(k)[1] * inner + y
+        arrived(te, w)
+        if inner == 2:
+            across(slot(te, w), far(k)[1]).start()
         over(slot(te, w), te).start()
 
-    def from_across(zo):
-        te = zo * inner + (inner - 1 - y)
-        arrived(te, w)
-        over(slot(te, w), te).start()
-
-    def both_sides(step, act_on):
-        @pl.when(z - step >= 0)
-        def _():
-            act_on(z - step)
-
-        @pl.when(z + step < outer)
-        def _():
-            act_on(z + step)
-
-    for step in range(1, outer):
-        @pl.when(z - step >= 0)
-        def _():
-            zo = z - step
-            te = zo * inner + y
+    def from_across(k):
+        if inner == 2:
+            te = (far(k)[1] if k else z) * inner + (inner - 1 - y)
             arrived(te, w)
-
-            @pl.when(z + 1 < outer)
-            def _():
-                up(slot(te, w), zo).start()
-
-            spread(zo)
-
-        @pl.when(z + step < outer)
-        def _():
-            zo = z + step
-            te = zo * inner + y
-            arrived(te, w)
-
-            @pl.when(z > 0)
-            def _():
-                down(slot(te, w), zo).start()
-
-            spread(zo)
-
-        if inner == 2:
-            if step == 1:
-                from_across(z)
-            else:
-                both_sides(step - 1, from_across)
-    if inner == 2:
-        if outer == 1:
-            from_across(z)
-        else:
-            both_sides(outer - 1, from_across)
-
-    def small(tw):
-        extra = xg[pl.ds(pl.multiple_of(tw * wave_rows, wave_rows), wave_rows), width:]
+            over(slot(te, w), te).start()
+
+    def wave_half(h):
+        @pl.loop(0, half_e)
+        def _(i):
+            arrived(h * half_e + i, peer)
+
+    def small(extra):
         lanes = extra.shape[1]
         src = lax.broadcasted_iota(jnp.int32, (lanes, LANES), 0)
         col = lax.broadcasted_iota(jnp.int32, (lanes, LANES), 1)
@@ -177,27 +148,31 @@
         pick += jnp.where(is_weight & ((src == own) | (src == own + experts)), 1.0, 0.0)
         return dot(extra, pick.astype(BF))
 
-    said = small(w)
-    lane = lax.broadcasted_iota(jnp.int32, (wave_rows, shard), 1).astype(F32)
-    first = (e * shard).astype(F32)
-    for q in range(books):
-        mem[:, q * shard:(q + 1) * shard] = jnp.where(
-            said[:, q:q + 1] - first == lane, 1.0, 0.0
-        ).astype(BF)
-    place = lax.broadcasted_iota(jnp.int32, (wave_rows, wave_rows), 1).astype(F32)
-    order = jnp.where(said[:, books:books + 1] == place, 1.0, 0.0).astype(BF)
-    loads[0].wait()
-    f_tile = min(channels, 512)
-
-    @pl.loop(0, channels // f_tile)
-    def _(n):
-        cols = pl.ds(pl.multiple_of(n * f_tile, f_tile), f_tile)
-        part = dot(mem[...], tabv[:, cols]).astype(BF)
-        fs[:, cols] = lax.dot_general(
-            order, part, (((0,), (0,)), ((), ())), preferred_element_type=F32
-        ).astype(BF)
-
-    turns = sorted(range(1, outer), key=lambda d: -min(d, outer - d)) + [0]
+    def frames():
+        said = small(jnp.concatenate([
+            xg[pl.ds(pl.multiple_of((h * n_w + w) * half_rows, half_rows), half_rows), width:]
+            for h in range(halves)
+        ], axis=0))
+        lane = lax.broadcasted_iota(jnp.int32, (wave_rows, shard), 1).astype(F32)
+        first = (e * shard).astype(F32)
+        for q in range(books):
+            mem[:, q * shard:(q + 1) * shard] = jnp.where(
+                said[:, q:q + 1] - first == lane, 1.0, 0.0
+            ).astype(BF)
+        place = lax.broadcasted_iota(jnp.int32, (wave_rows, wave_rows), 1).astype(F32)
+        order = jnp.where(said[:, books:books + 1] == place, 1.0, 0.0).astype(BF)
+        loads[0].wait()
+        f_tile = min(channels, 512)
+
+        @pl.loop(0, channels // f_tile)
+        def _(n):
+            cols = pl.ds(pl.multiple_of(n * f_tile, f_tile), f_tile)
+            part = dot(mem[...], tabv[:, cols]).astype(BF)
+            fs[:, cols] = lax.dot_general(
+                order, part, (((0,), (0,)), ((), ())), preferred_element_type=F32
+            ).astype(BF)
+
+    turns = list(range(outer - 1, -1, -1))
 
     def block(zo, yo):
         return pl.ds(pl.multiple_of((zo * inner + yo) * rows, rows), rows)
@@ -209,17 +184,17 @@
         return remote(src.at[block(zo, 1 - y), :], dst.at[zrows(zo), :], ss.at[zo], rs.at[zo], ye, w)
 
     def z_copy(src, dst, ss, rs, d):
-        zo = (z + d) % outer
+        zo = far(d)[0] if d else z
         return remote(src.at[zrows(zo), :], dst.at[zrows(d - 1), :], ss.at[d - 1], rs.at[d - 1], zo * inner + y, w)
 
     def f_start():
         if inner == 2:
             for d in turns:
-                y_copy(fs, fy, fys, fyr, (z + d) % outer).start()
+                y_copy(fs, fy, fys, fyr, far(d)[0] if d else z).start()
 
     def f_middle():
         for d in turns:
-            zo = (z + d) % outer
+            zo = far(d)[0] if d else z
             total = fs[block(zo, y), :].astype(F32)
             if inner == 2:
                 y_copy(fs, fy, fys, fyr, zo).wait_recv()
@@ -230,56 +205,94 @@
             else:
                 fr_ref[...] = total
 
-    f_start()
-
-    def chunk(tw, dst):
-        x = xg[pl.ds(pl.multiple_of(tw * wave_rows, wave_rows), wave_rows), :width]
-        told = small(tw)
-        for j in range(local):
-            gu = dot(x, wgu[j])
+    def gate_up(h, j):
+        mine = pl.ds(pl.multiple_of(h * (n_w * half_rows), n_w * half_rows), n_w * half_rows)
+        told = small(xg[mine, width:])
+        if True:
+            gu = dot(xg[mine, :width], wgu[j])
             g = gu[:, :units]
             u = gu[:, units:]
             a = g / (1.0 + jnp.exp(-g)) * u * told[:, books + 1 + j:books + 2 + j]
             act[:, j * units:(j + 1) * units] = a.astype(BF)
+
+    def down(h):
         tile = min(width, 512)
+        at = [pl.ds(pl.multiple_of((tw * halves + h) * half_rows, half_rows), half_rows) for tw in range(n_w)]
 
         @pl.loop(0, width // tile)
         def _(n):
             cols = pl.ds(pl.multiple_of(n * tile, tile), tile)
-            dst[:, cols] = dot(act[...], wdv[:, cols]).astype(BF)
-
-    @pl.loop(0, n_e)
-    def _(te):
-        arrived(te, peer)
-
+            out = dot(act[...], wdv[:, cols]).astype(BF)
+            for tw in range(n_w):
+                part[at[tw], cols] = out[tw * half_rows:(tw + 1) * half_rows]
+
+    def swap(h, i):
+        rows_out = pl.ds(pl.multiple_of((peer * halves + h) * half_rows, half_rows), half_rows)
+        rows_in = pl.ds(pl.multiple_of(h * half_rows, half_rows), half_rows)
+        return remote(part.at[rows_out, :], precv.at[rows_in, :], p_sem.at[2 * i], p_sem.at[2 * i + 1], e, peer)
+
+    def paired(zo, yo):
+        own = pl.ds(pl.multiple_of(w * wave_rows + (zo * inner + yo) * rows, rows), rows)
+        return part[own, :].astype(F32) + precv[block(zo, yo), :].astype(F32)
+
+    def y_start(ks):
+        if inner == 2:
+            for k in ks:
+                zo = far(k)[0] if k else z
+                ps[block(zo, 1 - y), :] = paired(zo, 1 - y).astype(BF)
+                y_copy(ps, my, mys, myr, zo).start()
+
+    def y_end(k):
+        zo = far(k)[0] if k else z
+        total = paired(zo, y)
+        if inner == 2:
+            y_copy(ps, my, mys, myr, zo).wait_recv()
+            total += my[zrows(zo), :].astype(F32)
+        if k == 0:
+            return total
+        ma[zrows(zo), :] = total.astype(BF)
+        z_copy(ma, mz, mzs, mzr, k).start()
+
+    per_half = outer // halves
+    near = list(range(per_half - 1, -1, -1))
+    away = list(range(outer - 1, per_half - 1, -1))
+    h_near = z // per_half
+    h_away = (h_near + 1) % halves
+    for k in range(1, per_half):
+        spread(k)
+        from_across(k - 1)
+    if halves == 2:
+        spread(per_half)
+    from_across(per_half - 1)
+    wave_half(h_near)
     for load in loads[1:]:
         load.wait()
-    chunk(peer, psend)
-    swap = remote(psend, precv, p_sem.at[0], p_sem.at[1], e, peer)
-    swap.start()
+    for j in range(local):
+        gate_up(h_near, j)
+    for k in range(per_half + 1, outer):
+        spread(k)
+        from_across(k - 1)
+    down(h_near)
+    swap(h_near, 0).start()
+    if halves == 2:
+        from_across(outer - 1)
+    swap(h_near, 0).wait_recv()
+    y_start(near)
+    frames()
+    f_start()
+    if halves == 2:
+        wave_half(h_away)
+        for j in range(local):
+            gate_up(h_away, j)
+        down(h_away)
+        swap(h_away, 1).start()
     f_middle()
-    chunk(w, pown)
-    swap.wait_recv()
-
-    if inner == 2:
-        for d in turns:
-            zo = (z + d) % outer
-            there = block(zo, 1 - y)
-            ps[there, :] = (pown[there, :].astype(F32) + precv[there, :].astype(F32)).astype(BF)
-            y_copy(ps, my, mys, myr, zo).start()
-    mine = None
-    for d in turns:
-        zo = (z + d) % outer
-        here = block(zo, y)
-        total = pown[here, :].astype(F32) + precv[here, :].astype(F32)
-        if inner == 2:
-            y_copy(ps, my, mys, myr, zo).wait_recv()
-            total += my[zrows(zo), :].astype(F32)
-        if d:
-            ma[zrows(zo), :] = total.astype(BF)
-            z_copy(ma, mz, mzs, mzr, d).start()
-        else:
-            mine = total
+    if halves == 2:
+        swap(h_away, 1).wait_recv()
+        y_start(away)
+    for k in near[:-1] + away:
+        y_end(k)
+    mine = y_end(0)
     for d in turns[:-1]:
         z_copy(fa, fz, fzs, fzr, d).wait_recv()
         fr_ref[...] += fz[zrows(d - 1), :].astype(F32)
@@ -289,19 +302,12 @@
     moe_ref[...] = mine.astype(BF)
 
     for zo in range(outer):
-        @pl.when((z + 1 < outer) & (zo <= z))
-        def _():
-            up(x_ref, zo).wait_send()
-
-        @pl.when((z > 0) & (zo >= z))
-        def _():
-            down(x_ref, zo).wait_send()
-
         if inner == 2:
             across(x_ref, zo).wait_send()
             y_copy(fs, fy, fys, fyr, zo).wait_send()
             y_copy(ps, my, mys, myr, zo).wait_send()
     for d in turns[:-1]:
+        along(d).wait_send()
         z_copy(fa, fz, fzs, fzr, d).wait_send()
         z_copy(ma, mz, mzs, mzr, d).wait_send()
 
@@ -309,7 +315,8 @@
     def _(te):
         over(x_ref, te).wait_send()
 
-    swap.wait_send()
+    for h in range(halves):
+        swap(h_near if h == 0 else h_away, h).wait_send()
 
 
 def exchange(packed, w_gate, w_up, w_down, table, width, experts, books):
@@ -317,6 +324,7 @@
     n_w = lax.axis_size("wave")
     inner = 2 if n_e % 2 == 0 else 1
     outer = n_e // inner
+    halves = 2 if outer > 1 and outer & (outer - 1) == 0 else 1
     rows = packed.shape[0]
     local, _, units = w_gate.shape
     channels = table.shape[1]
@@ -330,9 +338,8 @@
         vm((local * units, width), BF),
         vm(table.shape, BF),
         vm((wave_rows, table.shape[0]), BF),
-        vm((wave_rows, local * units), BF),
-        vm((wave_rows, width), BF),
-        vm((wave_rows, width), BF),
+        vm((n_w * wave_rows // halves, local * units), BF),
+        vm((n_w * wave_rows, width), BF),
         vm((wave_rows, width), BF),
         vm((wave_rows, width), BF),
         vm((outer * rows, width), BF),
@@ -342,14 +349,14 @@
         vm((outer * rows, channels), BF),
         vm((outer * rows, channels), BF),
         vm((hops * rows, channels), BF),
-        dma(2 + 2 * local), dma(outer), dma(outer), dma(outer), dma(n_e), dma(n_w * n_e),
-        dma(2), dma(outer), dma(outer), dma(hops), dma(hops),
+        dma(2 + 2 * local), dma(outer), dma(outer), dma(n_e), dma(n_w * n_e),
+        dma(4), dma(outer), dma(outer), dma(hops), dma(hops),
         dma(outer), dma(outer), dma(hops), dma(hops),
     ]
     any_spec = pl.BlockSpec(memory_space=pl.ANY)
     vm_spec = pl.BlockSpec(memory_space=pltpu.VMEM)
     return pl.pallas_call(
-        functools.partial(kernel, n_e, n_w, inner, experts, books, None),
+        functools.partial(kernel, n_e, n_w, inner, experts, books),
         out_shape=(
             jax.ShapeDtypeStruct((rows, width), BF),
             jax.ShapeDtypeStruct((rows, channels), F32),

time: 59.9 us -> 65 us (1.085)
  Pallas kernels: 49 us -> 54 us
    pallas_call x1, Pallas kernels: 49 us -> 54 us  [exchange(): pl.pallas_call(functools.partial(kernel, n_e, n_w, inner, experts, books)...]
where the time goes in v2:
time: 65 us; the launch traced here: 64.7 us
  Pallas kernels  54 us (83%)
  local copies, waits for them, and re-layouts  7.21 us (11%)
  other arithmetic  2.4 us (4%)
  between operations  0.75 us (1%)
    pallas_call x1, Pallas kernels, exchange(): pl.pallas_call(functools.partial(kernel, n_e, n_w, inner, experts, books)...  54 us
    reshape x1, local copies, waits for them, and re-layouts, per_device(): return (moe.reshape(sessions, steps, width), samples, carried)  1.66 us
    unnamed x10, local copies, waits for them, and re-layouts  1.58 us

profile of v2, /device:TPU:0, one launch (start us, length us, event | category | flops | bytes accessed | tf_op | source)
XLA Modules:
  0.0 64.7 jit_solution(12708338630265810485)
XLA Ops:
  0.6 0.0 copy-start
  0.6 1.0 %reshape.201 = bf16[32,2048]{1,0:T(8,128)(2,1)S(1)} reshape(bf16[16,2,2048]{2,1,0:T(2,128)(2,1)} %param.13) | data formatting | bytes 262144 | tf_op jit(solution)/shard_map/reshape | solution.py:407
  1.7 0.8 %copy.46 = f32[16,2,8]{2,1,0:T(2,128)S(1)} copy(f32[16,2,8]{0,2,1:T(8,128)} %param.15) | data formatting | bytes 2048 | tf_op args[2]
  2.5 0.1 copy.47
  2.5 0.8 %copy.44 = s32[16,2,8]{2,1,0:T(2,128)S(1)} copy(s32[16,2,8]{0,2,1:T(8,128)} %param.14) | data formatting | bytes 2048 | tf_op args[1]
  3.3 0.1 copy.45
  3.4 0.1 copy.49
  3.5 0.1 copy.48
  3.6 0.7 %fusion.18 = (bf16[32,16]{1,0:T(8,128)(2,1)S(1)}, bf16[32,16]{1,0:T(8,128)(2,1)S(1)}) fusion(s32[32,16]{1,0:T(8,128)} %bitcast.25), kind=kLoop, calls=%fused_computation.40 | loop fusion | flops 10752 | bytes 4096 | tf_op jit(solution)/shard_map/convert_element_type | solution.py:400
  4.3 0.7 %fusion.26 = s32[16]{0:T(128)S(1)} fusion(s32[16]{0:T(128)} %param.20), kind=kLoop, calls=%fused_computation.61 | loop fusion | flops 592 | bytes 128 | tf_op jit(solution)/shard_map/mul | solution.py:392
  5.0 0.1 iota_add_fusion
  5.1 0.1 add.130
  5.2 0.8 %concatenate.6.x_ref = bf16[32,2176]{1,0:T(8,128)(2,1)} concatenate(bf16[32,2048]{1,0:T(8,128)(2,1)S(1)} %reshape.201, bf16[32,16]{1,0:T(8,128)(2,1)S(1)} %get-tuple-element.19, bf16[32,16]{1,0:T(8,128)(2,1)S(1)} %get-tuple-element.18, bf16[32,16]{1,0:T(8,128)(2,1)S(1)} %get-tuple-element.17, bf16[32,16]{1,0:T(8,128)(2,1)S(1)} %get-tuple-element.16, ...), dimensions={1} | concatenate | bytes 278528 | tf_op jit(solution)/shard_map/concatenate | solution.py:407
  6.0 54.0 %shard_map.148 = (bf16[32,2048]{1,0:T(8,128)(2,1)}, f32[32,1024]{1,0:T(8,128)}) custom-call(bf16[32,2176]{1,0:T(8,128)(2,1)} %concatenate.6.x_ref, bf16[2,2048,384]{2,1,0:T(8,128)(2,1)} %wg_ref.1, bf16[2,2048,384]{2,1,0:T(8,128)(2,1)} %wu_ref.1, bf16[768,2048]{1,0:T(8,128)(2,1)} %bitcast.15, bf16[2048,1024]{1,0:T(8,128)(2,1)} %bitcast.14), custom_call_target="tpu_custom_call" | custom-call | tf_op jit(solution)/shard_map/pallas_call | solution.py:358
  60.0 1.7 %reshape.205 = bf16[16,2,2048]{2,1,0:T(2,128)(2,1)} reshape(bf16[32,2048]{1,0:T(8,128)(2,1)} %get-tuple-element.5) | data formatting | bytes 262144 | tf_op jit(solution)/shard_map/reshape | solution.py:422
  61.7 0.0 copy-done.1
  61.7 1.0 %reshape.206 = f32[16,2,1024]{2,1,0:T(2,128)S(1)} reshape(f32[32,1024]{1,0:T(8,128)} %get-tuple-element.6) | data formatting | bytes 262144 | tf_op jit(solution)/shard_map/reshape | solution.py:412
  62.7 0.0 copy-done.2
  62.8 0.1 fusion.8
  62.9 0.1 copy.57
  63.0 0.0 copy-done
  63.0 0.3 convolution_convert_fusion
  63.3 0.7 %reshape.208 = bf16[16,2,512]{2,1,0:T(2,128)(2,1)} reshape(bf16[32,512]{1,0:T(8,128)(2,1)S(1)} %convolution_convert_fusion) | data formatting | bytes 65536 | tf_op jit(solution)/shard_map/reshape | solution.py:420
  64.0 0.7 %fusion = bf16[16,6,1024]{2,0,1:T(8,128)(2,1)} fusion(f32[16,2,1024]{2,0,1:T(8,128)S(1)} %copy.55, f32[16,6,1024]{2,0,1:T(8,128)S(1)} %convert_element_type.50), kind=kLoop, calls=%fused_computation.4 | loop fusion | flops 98304 | bytes 720896 | tf_op jit(solution)/shard_map/convert
  (13 shorter events, 0.2 us)
Async XLA Ops:
  0.6 62.4 %copy-start = (bf16[1024,512]{1,0:T(8,128)(2,1)S(1)}, bf16[1024,512]{1,0:T(8,128)(2,1)}, u32[]{:S(2)}) copy-start(bf16[1024,512]{1,0:T(8,128)(2,1)} %param.25) | copy-start | bytes 3145732
  6.0 55.7 %copy-start.1 = (bf16[16,6,1024]{2,0,1:T(8,128)(2,1)S(1)}, bf16[16,6,1024]{2,0,1:T(8,128)(2,1)}, u32[]{:S(2)}) copy-start(bf16[16,6,1024]{2,0,1:T(8,128)(2,1)} %param.22) | copy-start | bytes 589828
  6.0 56.8 %copy-start.2 = (f32[7,1024]{1,0:T(8,128)S(1)}, f32[7,1024]{1,0:T(8,128)}, u32[]{:S(2)}) copy-start(f32[7,1024]{1,0:T(8,128)} %param.23) | copy-start | bytes 86020
  6.0 56.8 %copy-start.3 = (f32[1024]{0:T(1024)S(1)}, f32[1024]{0:T(1024)}, u32[]{:S(2)}) copy-start(f32[1024]{0:T(1024)} %param.24) | copy-start | bytes 12292

commit v3 on v1

--- a/solution.py
+++ b/solution.py
@@ -19,19 +19,20 @@
 
 
 def kernel(
-    n_e, n_w, inner, experts, books, scales,
-    x_ref, wg_ref, wu_ref, wd_ref, tab_ref,
-    moe_ref, fr_ref,
-    xg, wgu, wdv, tabv, mem, act,
+    n_e, n_w, inner, experts, books,
+    h_ref, id_ref, rw_ref, co_ref, ow_ref, st_ref, tap_ref, bias_ref, us_ref,
+    wg_ref, wu_ref, wd_ref, tab_ref,
+    moe_ref, wave_ref, new_ref,
+    stage, early, xg, wgu, wdv, tabv, mem, act,
     psend, precv, pown, ps, my, ma, mz,
-    fs, fy, fa, fz,
+    fs, fy, fa, fz, fr_ref,
     w_sem, zu_sem, zd_sem, ys_sem, ws_sem, ag_recv,
     p_sem, mys, myr, mzs, mzr, fys, fyr, fzs, fzr,
 ):
     outer = n_e // inner
-    rows = x_ref.shape[0]
-    width = moe_ref.shape[1]
-    channels = fr_ref.shape[1]
+    sessions, steps, width = h_ref.shape
+    rows = sessions * steps
+    channels = tab_ref.shape[1]
     local = wg_ref.shape[0]
     units = wg_ref.shape[2]
     shard = tab_ref.shape[0] // books
@@ -56,6 +57,45 @@
         loads.append(pltpu.make_async_copy(wu_ref.at[j], wgu.at[j, :, pl.ds(units, units)], w_sem.at[2 + 2 * j]))
     loads.append(pltpu.make_async_copy(wd_ref, wdv, w_sem.at[1 + 2 * local]))
 
+    lanes = stage.shape[1] - width
+    lane_i = lax.broadcasted_iota(jnp.int32, (sessions, lanes), 1)
+    eye = lax.broadcasted_iota(jnp.int32, (sessions, sessions), 0) == lax.broadcasted_iota(
+        jnp.int32, (sessions, sessions), 1
+    )
+    owner = jnp.sum(
+        jnp.where(eye, jnp.broadcast_to(ow_ref[...].astype(F32), (sessions, sessions)), 0.0),
+        axis=1, keepdims=True,
+    )
+    holder = jnp.floor((owner + 0.5) / sessions)
+    within = owner - holder * sessions
+    holder = jnp.floor((holder + 0.5) / n_w)
+    code_at = 2 * experts
+    dest_at = code_at + 2 * books
+    hid = h_ref[...]
+    for t in range(steps):
+        ids = id_ref[:, t, :]
+        rw = rw_ref[:, t, :]
+        co = co_ref[:, t, :].astype(F32)
+        both = jnp.zeros((sessions, lanes), F32)
+        for k in range(ids.shape[1]):
+            named = ids[:, k:k + 1]
+            both += jnp.where((named == lane_i) | (named + experts == lane_i), rw[:, k:k + 1], 0.0)
+        high = both.astype(BF).astype(F32)
+        extra = jnp.where(lane_i < experts, high, both - high)
+        extra = jnp.where(lane_i < code_at, extra, 0.0)
+        for q in range(books):
+            c = co[:, q:q + 1]
+            top = jnp.floor((c + 0.5) / RADIX)
+            extra = jnp.where(lane_i == code_at + q, top, extra)
+            extra = jnp.where(lane_i == code_at + books + q, c - top * RADIX, extra)
+        dest = holder * rows + t * sessions + within
+        top = jnp.floor((dest + 0.5) / RADIX)
+        extra = jnp.where(lane_i == dest_at, top, extra)
+        extra = jnp.where(lane_i == dest_at + 1, dest - top * RADIX, extra)
+        stage[t * sessions:(t + 1) * sessions, :width] = hid[:, t, :]
+        stage[t * sessions:(t + 1) * sessions, width:] = extra.astype(BF)
+    x_ref = stage
+
     barrier = pltpu.get_barrier_semaphore()
 
     def greet(te, tw):
@@ -103,6 +143,17 @@
     for load in loads:
         load.start()
     xg[pl.ds((w * n_e + e) * rows, rows), :] = x_ref[...]
+
+    state_len = st_ref.shape[1]
+    taps = tap_ref.shape[0]
+    state = st_ref[...]
+    for t in range(steps):
+        total = jnp.broadcast_to(bias_ref[...], (sessions, channels))
+        for j in range(t + 1, taps):
+            total += tap_ref[j:j + 1, :] * state[:, state_len + t - j, :].astype(F32)
+        early[t * sessions:(t + 1) * sessions, :] = total
+    for i in range(state_len - steps):
+        new_ref[:, i, :] = state[:, i + steps, :]
 
     def spread(zo):
         te = zo * inner + y
@@ -283,10 +334,22 @@
     for d in turns[:-1]:
         z_copy(fa, fz, fzs, fzr, d).wait_recv()
         fr_ref[...] += fz[zrows(d - 1), :].astype(F32)
+    got = [fr_ref[t * sessions:(t + 1) * sessions, :] for t in range(steps)]
+    decoded = []
+    for t in range(steps):
+        total = early[t * sessions:(t + 1) * sessions, :]
+        for j in range(t + 1):
+            total += tap_ref[j:j + 1, :] * got[t - j]
+        decoded.append(jax.nn.gelu(total).astype(BF))
+        new_ref[:, state_len - steps + t, :] = got[t].astype(BF)
+    samples = dot(jnp.concatenate(decoded, axis=0), us_ref[...]).astype(BF)
+    for t in range(steps):
+        wave_ref[:, t, :] = samples[t * sessions:(t + 1) * sessions]
     for d in turns[:-1]:
         z_copy(ma, mz, mzs, mzr, d).wait_recv()
         mine += mz[zrows(d - 1), :].astype(F32)
-    moe_ref[...] = mine.astype(BF)
+    for t in range(steps):
+        moe_ref[:, t, :] = mine[t * sessions:(t + 1) * sessions].astype(BF)
 
     for zo in range(outer):
         @pl.when((z + 1 < outer) & (zo <= z))
@@ -312,12 +375,15 @@
     swap.wait_send()
 
 
-def exchange(packed, w_gate, w_up, w_down, table, width, experts, books):
+def exchange(small_args, w_gate, w_up, w_down, table, experts, books):
     n_e = lax.axis_size("expert")
     n_w = lax.axis_size("wave")
     inner = 2 if n_e % 2 == 0 else 1
     outer = n_e // inner
-    rows = packed.shape[0]
+    sessions, steps, width = small_args[0].shape
+    rows = sessions * steps
+    used = 2 * experts + 2 * books + 2
+    across = width + used + -used % LANES
     local, _, units = w_gate.shape
     channels = table.shape[1]
     wave_rows = n_e * rows
@@ -325,7 +391,9 @@
     dma = lambda *s: pltpu.SemaphoreType.DMA(s)
     hops = max(outer - 1, 1)
     scratch = [
-        vm((n_w * wave_rows, packed.shape[1]), BF),
+        vm((rows, across), BF),
+        vm((rows, channels), F32),
+        vm((n_w * wave_rows, across), BF),
         vm((local, width, 2 * units), BF),
         vm((local * units, width), BF),
         vm(table.shape, BF),
@@ -342,6 +410,7 @@
         vm((outer * rows, channels), BF),
         vm((outer * rows, channels), BF),
         vm((hops * rows, channels), BF),
+        vm((rows, channels), F32),
         dma(2 + 2 * local), dma(outer), dma(outer), dma(outer), dma(n_e), dma(n_w * n_e),
         dma(2), dma(outer), dma(outer), dma(hops), dma(hops),
         dma(outer), dma(outer), dma(hops), dma(hops),
@@ -349,18 +418,19 @@
     any_spec = pl.BlockSpec(memory_space=pl.ANY)
     vm_spec = pl.BlockSpec(memory_space=pltpu.VMEM)
     return pl.pallas_call(
-        functools.partial(kernel, n_e, n_w, inner, experts, books, None),
+        functools.partial(kernel, n_e, n_w, inner, experts, books),
         out_shape=(
-            jax.ShapeDtypeStruct((rows, width), BF),
-            jax.ShapeDtypeStruct((rows, channels), F32),
+            jax.ShapeDtypeStruct((sessions, steps, width), BF),
+            jax.ShapeDtypeStruct((sessions, steps, small_args[8].shape[1]), BF),
+            jax.ShapeDtypeStruct(small_args[5].shape, BF),
         ),
-        in_specs=[vm_spec] + [any_spec] * 4,
-        out_specs=(vm_spec, vm_spec),
+        in_specs=[vm_spec] * len(small_args) + [any_spec] * 4,
+        out_specs=(vm_spec, vm_spec, vm_spec),
         scratch_shapes=scratch,
         compiler_params=pltpu.CompilerParams(
             collective_id=0, has_side_effects=True, vmem_limit_bytes=60 * 1024 * 1024
         ),
-    )(packed, w_gate, w_up, w_down, table)
+    )(*small_args, w_gate, w_up, w_down, table)
 
 
 def per_device(
@@ -368,51 +438,17 @@
     codes, owner_slot, code_table, conv_state, conv_taps, conv_bias, upsample,
 ):
     n_e = lax.axis_size("expert")
-    n_w = lax.axis_size("wave")
-    sessions, steps, width = hidden_rows.shape
-    rows = sessions * steps
-    top = expert_ids.shape[2]
+    width = hidden_rows.shape[2]
     experts = n_e * w_gate.shape[0]
     books, shard, channels = code_table.shape
-
-    ids = expert_ids.reshape(rows, top)
-    names = jnp.arange(experts, dtype=jnp.int32)
-    weight = jnp.sum(
-        jnp.where(ids[:, :, None] == names, route_weights.reshape(rows, top, 1), 0.0), axis=1
+    return exchange(
+        (
+            hidden_rows, expert_ids, route_weights, codes, owner_slot.reshape(1, -1),
+            conv_state, conv_taps, conv_bias.reshape(1, -1), upsample,
+        ),
+        w_gate, w_up, w_down.reshape(-1, width), code_table.reshape(books * shard, channels),
+        experts, books,
     )
-    high = lax.reduce_precision(weight, 8, 7)
-    dest = owner_slot // sessions // n_w * sessions + owner_slot % sessions
-    dest = (dest[:, None] * steps + jnp.arange(steps, dtype=jnp.int32)).reshape(rows, 1)
-    code_rows = codes.reshape(rows, books)
-    used = 2 * experts + 2 * books + 2
-    extra = jnp.concatenate(
-        [
-            high.astype(BF),
-            (weight - high).astype(BF),
-            (code_rows // RADIX).astype(BF),
-            (code_rows % RADIX).astype(BF),
-            (dest // RADIX).astype(BF),
-            (dest % RADIX).astype(BF),
-            jnp.zeros((rows, -used % LANES), BF),
-        ],
-        axis=1,
-    )
-    packed = jnp.concatenate([hidden_rows.reshape(rows, width), extra], axis=1)
-    moe, frames = exchange(
-        packed, w_gate, w_up, w_down.reshape(-1, width),
-        code_table.reshape(books * shard, channels), width, experts, books,
-    )
-    frames = frames.reshape(sessions, steps, channels)
-    history = jnp.concatenate([conv_state.astype(F32), frames], axis=1)
-    state_len = conv_state.shape[1]
-    filtered = jnp.broadcast_to(conv_bias, frames.shape)
-    for offset in range(conv_taps.shape[0]):
-        filtered = filtered + conv_taps[offset] * history[:, state_len - offset:state_len - offset + steps]
-    decoded = jax.nn.gelu(filtered).astype(BF)
-    samples = jnp.dot(decoded.reshape(rows, channels), upsample, preferred_element_type=F32)
-    samples = samples.astype(BF).reshape(sessions, steps, upsample.shape[1])
-    carried = history[:, steps:].astype(BF)
-    return moe.reshape(sessions, steps, width), samples, carried
 
 
 def solution(mesh):

time: 59.9 us -> 61.8 us (1.032)
  Pallas kernels: 49 us -> 51.5 us
  other arithmetic: 2.4 us -> 0 us
  local copies, waits for them, and re-layouts: 7.21 us -> 9.27 us
    unnamed x10 -> x5, local copies, waits for them, and re-layouts: 1.58 us -> 7.53 us
    reshape x6 -> x0, local copies, waits for them, and re-layouts: 4.41 us -> none  [the longest x1 1.66 us: per_device(): return (moe.reshape(sessions, steps, width), samples, carried)]
    pallas_call x1, Pallas kernels: 49 us -> 51.5 us  [exchange(): pl.pallas_call(functools.partial(kernel, n_e, n_w, inner, experts, books)...]
    pallas_call x0 -> x1, local copies, waits for them, and re-layouts: none -> 1.74 us  [exchange(): pl.pallas_call(functools.partial(kernel, n_e, n_w, inner, experts, books)...]
    convert_element_type x5 -> x0, other arithmetic: 0.93 us -> none  [the longest x1 0.74 us: per_device(): (code_rows % RADIX).astype(BF)]
    concatenate x1 -> x0, local copies, waits for them, and re-layouts: 0.76 us -> none  [per_device(): packed = jnp.concatenate([hidden_rows.reshape(rows, width), extra], axis=1)]
    another operation x1 -> x0, other arithmetic: 0.7 us -> none
    mul x1 -> x0, other arithmetic: 0.68 us -> none  [per_device(): dest[:, None] * steps + jnp.arange(steps, dtype=jnp.int32)]
where the time goes in v3:
time: 61.8 us; the launch traced here: 61.4 us
  Pallas kernels  51.5 us (83%)
  local copies, waits for them, and re-layouts  9.27 us (15%)
  between operations  0.64 us (1%)
    pallas_call x1, Pallas kernels, exchange(): pl.pallas_call(functools.partial(kernel, n_e, n_w, inner, experts, books)...  51.5 us
    unnamed x5, local copies, waits for them, and re-layouts  7.53 us
    pallas_call x1, local copies, waits for them, and re-layouts, exchange(): pl.pallas_call(functools.partial(kernel, n_e, n_w, inner, experts, books)...  1.74 us

profile of v3, /device:TPU:0, one launch (start us, length us, event | category | flops | bytes accessed | tf_op | source)
XLA Modules:
  0.0 61.4 jit_solution(11833122716899802885)
XLA Ops:
  0.6 1.4 %copy.16.id_ref = s32[16,2,8]{2,1,0:T(2,128)} copy(s32[16,2,8]{0,2,1:T(8,128)} %param.14) | data formatting | bytes 2048 | tf_op args[1]
  2.0 1.4 %copy.17.rw_ref = f32[16,2,8]{2,1,0:T(2,128)} copy(f32[16,2,8]{0,2,1:T(8,128)} %param.15) | data formatting | bytes 2048 | tf_op args[2]
  3.4 1.7 %copy.18.st_ref = bf16[16,6,1024]{2,1,0:T(8,128)(2,1)} copy(bf16[16,6,1024]{2,0,1:T(8,128)(2,1)} %param.22) | data formatting | bytes 393216 | tf_op args[9]
  5.1 51.5 %shard_map.148 = (bf16[16,2,2048]{2,1,0:T(2,128)(2,1)}, bf16[16,2,512]{2,1,0:T(2,128)(2,1)}, bf16[16,6,1024]{2,1,0:T(8,128)(2,1)}) custom-call(bf16[16,2,2048]{2,1,0:T(2,128)(2,1)} %h_ref.1, s32[16,2,8]{2,1,0:T(2,128)} %copy.16.id_ref, f32[16,2,8]{2,1,0:T(2,128)} %copy.17.rw_ref, s32[16,2,16]{2,1,0:T(2,128)} %co_ref.1, s32[1,16]{1,0:T(1,128)} %bitcast.7, ...), custom_call_target="tpu_custom_call" | custom-call | tf_op jit(solution)/shard_map/pallas_call | solution.py:420
  56.7 1.7 %copy.19 = bf16[16,6,1024]{2,0,1:T(8,128)(2,1)} copy(bf16[16,6,1024]{2,1,0:T(8,128)(2,1)} %get-tuple-element.5) | data formatting | bytes 393216 | tf_op jit(solution)/shard_map/pallas_call | solution.py:420
  58.4 1.6 %copy.22 = bf16[16,2,2048]{2,1,0:T(2,128)(2,1)} copy(bf16[16,2,2048]{2,1,0:T(2,128)(2,1)} %get-tuple-element.9) | data formatting | bytes 262144
  60.1 1.4 %copy.23 = bf16[16,2,512]{2,1,0:T(2,128)(2,1)} copy(bf16[16,2,512]{2,1,0:T(2,128)(2,1)} %get-tuple-element.10) | data formatting | bytes 65536

commit v4 on v3

--- a/solution.py
+++ b/solution.py
@@ -62,10 +62,13 @@
     eye = lax.broadcasted_iota(jnp.int32, (sessions, sessions), 0) == lax.broadcasted_iota(
         jnp.int32, (sessions, sessions), 1
     )
-    owner = jnp.sum(
-        jnp.where(eye, jnp.broadcast_to(ow_ref[...].astype(F32), (sessions, sessions)), 0.0),
-        axis=1, keepdims=True,
-    )
+    lane_f = lane_i.astype(F32)
+
+    def column(row):
+        square = jnp.broadcast_to(row.astype(F32), (sessions, sessions))
+        return jnp.sum(jnp.where(eye, square, 0.0), axis=1, keepdims=True)
+
+    owner = column(ow_ref[...])
     holder = jnp.floor((owner + 0.5) / sessions)
     within = owner - holder * sessions
     holder = jnp.floor((holder + 0.5) / n_w)
@@ -73,13 +76,13 @@
     dest_at = code_at + 2 * books
     hid = h_ref[...]
     for t in range(steps):
-        ids = id_ref[:, t, :]
-        rw = rw_ref[:, t, :]
         co = co_ref[:, t, :].astype(F32)
         both = jnp.zeros((sessions, lanes), F32)
-        for k in range(ids.shape[1]):
-            named = ids[:, k:k + 1]
-            both += jnp.where((named == lane_i) | (named + experts == lane_i), rw[:, k:k + 1], 0.0)
+        for k in range(id_ref.shape[1]):
+            named = column(id_ref[t, k:k + 1, :])
+            both += jnp.where(
+                (named == lane_f) | (named + experts == lane_f), column(rw_ref[t, k:k + 1, :]), 0.0
+            )
         high = both.astype(BF).astype(F32)
         extra = jnp.where(lane_i < experts, high, both - high)
         extra = jnp.where(lane_i < code_at, extra, 0.0)
@@ -144,16 +147,15 @@
         load.start()
     xg[pl.ds((w * n_e + e) * rows, rows), :] = x_ref[...]
 
-    state_len = st_ref.shape[1]
+    state_len = st_ref.shape[0]
     taps = tap_ref.shape[0]
-    state = st_ref[...]
     for t in range(steps):
         total = jnp.broadcast_to(bias_ref[...], (sessions, channels))
         for j in range(t + 1, taps):
-            total += tap_ref[j:j + 1, :] * state[:, state_len + t - j, :].astype(F32)
+            total += tap_ref[j:j + 1, :] * st_ref[state_len + t - j].astype(F32)
         early[t * sessions:(t + 1) * sessions, :] = total
     for i in range(state_len - steps):
-        new_ref[:, i, :] = state[:, i + steps, :]
+        new_ref[i] = st_ref[i + steps]
 
     def spread(zo):
         te = zo * inner + y
@@ -341,7 +343,7 @@
         for j in range(t + 1):
             total += tap_ref[j:j + 1, :] * got[t - j]
         decoded.append(jax.nn.gelu(total).astype(BF))
-        new_ref[:, state_len - steps + t, :] = got[t].astype(BF)
+        new_ref[state_len - steps + t] = got[t].astype(BF)
     samples = dot(jnp.concatenate(decoded, axis=0), us_ref[...]).astype(BF)
     for t in range(steps):
         wave_ref[:, t, :] = samples[t * sessions:(t + 1) * sessions]
@@ -373,6 +375,12 @@
         over(x_ref, te).wait_send()
 
     swap.wait_send()
+
+
+def hand_over(a_ref, b_ref, c_ref, a_out, b_out, c_out):
+    a_out[...] = a_ref[...]
+    b_out[...] = b_ref[...]
+    c_out[...] = c_ref[...]
 
 
 def exchange(small_args, w_gate, w_up, w_down, table, experts, books):
@@ -441,14 +449,22 @@
     width = hidden_rows.shape[2]
     experts = n_e * w_gate.shape[0]
     books, shard, channels = code_table.shape
-    return exchange(
+    results = exchange(
         (
-            hidden_rows, expert_ids, route_weights, codes, owner_slot.reshape(1, -1),
-            conv_state, conv_taps, conv_bias.reshape(1, -1), upsample,
+            hidden_rows, expert_ids.transpose(1, 2, 0), route_weights.transpose(1, 2, 0), codes,
+            owner_slot.reshape(1, -1), conv_state.transpose(1, 0, 2), conv_taps, conv_bias.reshape(1, -1), upsample,
         ),
         w_gate, w_up, w_down.reshape(-1, width), code_table.reshape(books * shard, channels),
         experts, books,
     )
+    vm_spec = pl.BlockSpec(memory_space=pltpu.VMEM)
+    moe, samples, carried = pl.pallas_call(
+        hand_over,
+        out_shape=tuple(jax.ShapeDtypeStruct(r.shape, r.dtype) for r in results),
+        in_specs=[vm_spec] * 3,
+        out_specs=(vm_spec,) * 3,
+    )(*results)
+    return moe, samples, carried.transpose(1, 0, 2)
 
 
 def solution(mesh):

time: 61.8 us -> 53.4 us (0.86)
  local copies, waits for them, and re-layouts: 9.27 us -> 0 us
  Pallas kernels: 51.5 us -> 52.6 us
    unnamed x5 -> x0, local copies, waits for them, and re-layouts: 7.53 us -> none
    pallas_call x0 -> x1, Pallas kernels: none -> 1.74 us  [per_device(): pl.pallas_call(hand_over, out_shape=tuple((jax.ShapeDtypeStruct(r.shape,...]
    pallas_call x1 -> x0, local copies, waits for them, and re-layouts: 1.74 us -> none  [exchange(): pl.pallas_call(functools.partial(kernel, n_e, n_w, inner, experts, books)...]
    pallas_call x1, Pallas kernels: 51.5 us -> 50.8 us  [exchange(): pl.pallas_call(functools.partial(kernel, n_e, n_w, inner, experts, books)...]
where the time goes in v4:
time: 53.4 us; the launch traced here: 53.2 us
  Pallas kernels  52.6 us (99%)
  between operations  0.64 us (1%)
    pallas_call x1, Pallas kernels, exchange(): pl.pallas_call(functools.partial(kernel, n_e, n_w, inner, experts, books)...  50.8 us
    pallas_call x1, Pallas kernels, per_device(): pl.pallas_call(hand_over, out_shape=tuple((jax.ShapeDtypeStruct(r.shape,...  1.74 us

profile of v4, /device:TPU:0, one launch (start us, length us, event | category | flops | bytes accessed | tf_op | source)
XLA Modules:
  0.0 53.2 jit_solution(8012605076595938149)
XLA Ops:
  0.6 50.8 %shard_map.148 = (bf16[16,2,2048]{2,1,0:T(2,128)(2,1)}, bf16[16,2,512]{2,1,0:T(2,128)(2,1)}, bf16[6,16,1024]{2,1,0:T(8,128)(2,1)}) custom-call(bf16[16,2,2048]{2,1,0:T(2,128)(2,1)} %h_ref.1, s32[2,8,16]{2,1,0:T(8,128)} %bitcast.11, f32[2,8,16]{2,1,0:T(8,128)} %bitcast.12, s32[16,2,16]{2,1,0:T(2,128)} %co_ref.1, s32[1,16]{1,0:T(1,128)} %bitcast.14, ...), custom_call_target="tpu_custom_call" | custom-call | tf_op jit(solution)/shard_map/pallas_call | solution.py:428
  51.5 1.7 %shard_map.149 = (bf16[16,2,2048]{2,1,0:T(2,128)(2,1)}, bf16[16,2,512]{2,1,0:T(2,128)(2,1)}, bf16[6,16,1024]{2,1,0:T(8,128)(2,1)}) custom-call(bf16[16,2,2048]{2,1,0:T(2,128)(2,1)} %get-tuple-element.9.a_ref, bf16[16,2,512]{2,1,0:T(2,128)(2,1)} %get-tuple-element.10.b_ref, bf16[6,16,1024]{2,1,0:T(8,128)(2,1)} %get-tuple-element.11.c_ref), custom_call_target="tpu_custom_call" | custom-call | tf_op jit(solution)/shard_map/pallas_call | solution.py:461
